TPU v7x, 128 devices: a whole 4x4x4 slice. The times are simulated.
128 devices in a mesh: nodes: 16 (over x, z), cols: 8 (over y, core).
Axes of the slice: x: 4, y: 4, z: 4, core: 2. Of those that a mesh axis runs over, the one named last changes fastest.
Arguments:
- node_feats: bfloat16 [32768, 256], P(('nodes', 'cols')), may hold values from -6 to 6
- tile_row: int32 [16, 2816], P('nodes', 'cols'), may hold values from 0 to 15, as said below
- tile_col: int32 [16, 2816], P('nodes', 'cols'), may hold values from 0 to 31
- tile_bits: int32 [16, 2816, 16, 128], P('nodes', 'cols'), may hold values from 0 to 255, as said below
- w_self: bfloat16 [256, 256], replicated, may hold values from -0.375 to 0.375
- w_neigh: bfloat16 [256, 256], replicated, may hold values from -1.5 to 1.5
- bias: float32 [256], replicated, may hold values from -3 to 3
- cotangent: bfloat16 [32768, 256], P(('nodes', 'cols')), may hold values from -6 to 6
Outputs:
- layer_out: bfloat16 [32768, 256], P(('nodes', 'cols'))
- feat_grad: bfloat16 [32768, 256], P(('nodes', 'cols'))
- self_grad: float32 [256, 256], replicated
- neigh_grad: float32 [256, 256], replicated
- bias_grad: float32 [256], replicated
Inputs may be any that keep to these rules, and one draw needn't show every extreme that they name: `tile_row`: destination row block of a tile within its nodes group; in every nodes group at least one block carries no tile. `tile_col`: source row block of a tile within its cols index; a block may carry several tiles. `tile_bits`: bit j of word (w, a) of a tile is its edge from destination row a to source column 8 w + j; bits above the eighth are zero; some destination rows have no edge in any tile.
All inputs are finite; a program needn't handle non-finite values.
Results may differ from a plain program's by a relative error of at most 0.0075.
Values may be sent and summed in bfloat16 or wider, within the bound.
No kernel may reach another device: no remote copies, remote signals or barrier semaphores. Data moves between devices by JAX's collectives and lax.ppermute only.
A program may use at most 64 MiB of HBM per device.

v0:
```python
import math
import jax
import jax.numpy as jnp
from jax import lax
from jax.sharding import PartitionSpec as P


def unpack_tiles(packed):
    shifts = jnp.arange(8, dtype=jnp.int32)
    edge_flags = jnp.right_shift(packed[:, :, None, :], shifts[None, None, :, None]) & 1
    return edge_flags.reshape(packed.shape[0], 128, 128)


def shards(node_feats, tile_row, tile_col, tile_bits, w_self, w_neigh, bias, cotangent):
    rows_dev = node_feats.shape[0]
    width_in = node_feats.shape[1]
    node_count = lax.axis_size("nodes")
    col_count = lax.axis_size("cols")
    per_dev = rows_dev // 128
    dest_count = col_count * per_dev
    source_count = node_count * per_dev
    tile_count = tile_row.shape[1]
    tile_group = math.gcd(tile_count, 32)
    group_count = tile_count // tile_group
    rows_here = tile_row[0].reshape(group_count, tile_group)
    cols_here = tile_col[0].reshape(group_count, tile_group)
    packed_here = tile_bits[0].reshape(group_count, tile_group, 16, 128)
    source = lax.all_gather(node_feats, "nodes", axis=0, tiled=True)
    source_blocks = source.reshape(source_count, 128, width_in)

    def forward_step(totals, tile_set):
        summed, degree = totals
        rows_blk, cols_blk, packed_blk = tile_set
        edge_flags = unpack_tiles(packed_blk)
        bits_blk = edge_flags.astype(jnp.bfloat16)
        picked = source_blocks[cols_blk]
        products = jnp.einsum("tba,tbf->taf", bits_blk, picked, preferred_element_type=jnp.float32)
        summed = summed.at[rows_blk].add(products)
        degree = degree.at[rows_blk].add(jnp.sum(edge_flags, axis=1).astype(jnp.float32))
        return ((summed, degree), None)

    initial = (
        jnp.zeros((dest_count, 128, width_in), jnp.float32),
        jnp.zeros((dest_count, 128), jnp.float32),
    )
    (partial_sum, degree_part), _ = lax.scan(
        forward_step, initial, (rows_here, cols_here, packed_here)
    )
    summed, degree = (
        lax.psum_scatter(
            partial_sum.reshape(dest_count * 128, width_in), "cols", scatter_dimension=0, tiled=True
        ),
        lax.psum_scatter(
            degree_part.reshape(dest_count * 128), "cols", scatter_dimension=0, tiled=True
        ),
    )
    degree = jnp.maximum(degree, 1.0)
    neigh_mean = (summed / degree[:, None]).astype(jnp.bfloat16)
    preact = (
        jnp.dot(node_feats, w_self, preferred_element_type=jnp.float32)
        + jnp.dot(neigh_mean, w_neigh, preferred_element_type=jnp.float32)
        + bias
    )
    sigmoid_pre = jax.nn.sigmoid(preact)
    layer_out = (preact * sigmoid_pre).astype(jnp.bfloat16)
    pre_grad = (
        cotangent.astype(jnp.float32) * sigmoid_pre * (1.0 + preact * (1.0 - sigmoid_pre))
    ).astype(jnp.bfloat16)
    self_term = jnp.dot(node_feats.T, pre_grad, preferred_element_type=jnp.float32)
    neigh_term = jnp.dot(neigh_mean.T, pre_grad, preferred_element_type=jnp.float32)
    bias_term = jnp.sum(pre_grad.astype(jnp.float32), axis=0)
    self_grad, neigh_grad, bias_grad = lax.psum(
        (self_term, neigh_term, bias_term), ("nodes", "cols")
    )
    mean_grad = (
        jnp.dot(pre_grad, w_neigh.T, preferred_element_type=jnp.float32) / degree[:, None]
    ).astype(jnp.bfloat16)
    dest_grad = lax.all_gather(mean_grad, "cols", axis=0, tiled=True)
    grad_blocks = dest_grad.reshape(dest_count, 128, width_in)

    def backward_step(src_grad, tile_set):
        rows_blk, cols_blk, packed_blk = tile_set
        bits_blk = unpack_tiles(packed_blk).astype(jnp.bfloat16)
        picked = grad_blocks[rows_blk]
        products = jnp.einsum("tba,taf->tbf", bits_blk, picked, preferred_element_type=jnp.float32)
        return (src_grad.at[cols_blk].add(products), None)

    src_total, _ = lax.scan(
        backward_step,
        jnp.zeros((source_count, 128, width_in), jnp.float32),
        (rows_here, cols_here, packed_here),
    )
    src_total = src_total.reshape(source_count * 128, width_in)
    src_grad = lax.psum_scatter(src_total, "nodes", scatter_dimension=0, tiled=True)
    feat_grad = (jnp.dot(pre_grad, w_self.T, preferred_element_type=jnp.float32) + src_grad).astype(
        jnp.bfloat16
    )
    return (layer_out, feat_grad, self_grad, neigh_grad, bias_grad)


def solution(mesh):
    return jax.shard_map(
        shards,
        mesh=mesh,
        in_specs=(
            P(("nodes", "cols"), None),
            P("nodes", "cols"),
            P("nodes", "cols"),
            P("nodes", "cols", None, None),
            P(),
            P(),
            P(),
            P(("nodes", "cols"), None),
        ),
        out_specs=(P(("nodes", "cols"), None), P(("nodes", "cols"), None), P(), P(), P()),
        check_vma=False,
    )
```

profile of v0, /device:TPU:0, one launch (start us, length us, event | category | flops | bytes accessed | tf_op | source)
XLA Modules:
  0.0 557.2 jit_solution(13627646105467495376)
XLA Ops:
  9.5 48.4 %all-gather.3.cloned.1.call-done = bf16[4096,256]{1,0:T(8,128)(2,1)} async-done(((bf16[256,256]{1,0:T(8,128)(2,1)}), bf16[4096,256]{1,0:T(8,128)(2,1)}) %all-gather.3.cloned.1.call-update) | async-done | bytes 2097168 | tf_op jit(solution)/shard_map/all_gather | solution.py:28
  58.1 182.1 %while.22 = (s32[]{:T(128)}, f32[16,128,256]{2,1,0:T(8,128)S(1)}, f32[16,128]{1,0:T(8,128)S(1)}, s32[11,32]{1,0:T(8,128)S(1)}, s32[11,32,16,128]{3,2,1,0:T(8,128...) while((s32[]{:T(128)}, f32[16,128,256]{2,1,0:T(8,128)S(1)}, ...), condition=%wide.region_4.5_spmd, body=%wide.region_0.4_spmd.sunk | while | flops 272635072 | bytes 24165348 | solution.py:46
  58.2 3.6 gather_fusion
  62.9 4.4 fusion.56
  67.2 6.5 %scatter_fusion = f32[16,128,256]{2,1,0:T(8,128)S(1)} fusion(f32[16,128,256]{2,1,0:T(8,128)S(1)} %get-tuple-element.232, s32[32]{0:T(128)S(1)} %get-tuple-element.213, f32[32,128,256]{2,1,0:T(8,128)} %fusion.56), kind=kCustom, calls=%fused_computation.2.clone.1 | custom fusion | flops 1048576 | bytes 12583040 | tf_op jit(solution)/shard_map/while/body/eval_jaxpr/scatter-add | solution.py:38
  74.7 3.6 gather_fusion
  79.4 4.4 fusion.56
  83.8 6.5 %scatter_fusion = f32[16,128,256]{2,1,0:T(8,128)S(1)} fusion(f32[16,128,256]{2,1,0:T(8,128)S(1)} %get-tuple-element.232, s32[32]{0:T(128)S(1)} %get-tuple-element.213, f32[32,128,256]{2,1,0:T(8,128)} %fusion.56), kind=kCustom, calls=%fused_computation.2.clone.1 | custom fusion | flops 1048576 | bytes 12583040 | tf_op jit(solution)/shard_map/while/body/eval_jaxpr/scatter-add | solution.py:38
  91.3 3.6 gather_fusion
  96.0 4.4 fusion.56
  100.4 6.5 %scatter_fusion = f32[16,128,256]{2,1,0:T(8,128)S(1)} fusion(f32[16,128,256]{2,1,0:T(8,128)S(1)} %get-tuple-element.232, s32[32]{0:T(128)S(1)} %get-tuple-element.213, f32[32,128,256]{2,1,0:T(8,128)} %fusion.56), kind=kCustom, calls=%fused_computation.2.clone.1 | custom fusion | flops 1048576 | bytes 12583040 | tf_op jit(solution)/shard_map/while/body/eval_jaxpr/scatter-add | solution.py:38
  107.9 3.6 gather_fusion
  112.5 4.4 fusion.56
  116.9 6.5 %scatter_fusion = f32[16,128,256]{2,1,0:T(8,128)S(1)} fusion(f32[16,128,256]{2,1,0:T(8,128)S(1)} %get-tuple-element.232, s32[32]{0:T(128)S(1)} %get-tuple-element.213, f32[32,128,256]{2,1,0:T(8,128)} %fusion.56), kind=kCustom, calls=%fused_computation.2.clone.1 | custom fusion | flops 1048576 | bytes 12583040 | tf_op jit(solution)/shard_map/while/body/eval_jaxpr/scatter-add | solution.py:38
  124.4 3.6 gather_fusion
  129.1 4.4 fusion.56
  133.5 6.5 %scatter_fusion = f32[16,128,256]{2,1,0:T(8,128)S(1)} fusion(f32[16,128,256]{2,1,0:T(8,128)S(1)} %get-tuple-element.232, s32[32]{0:T(128)S(1)} %get-tuple-element.213, f32[32,128,256]{2,1,0:T(8,128)} %fusion.56), kind=kCustom, calls=%fused_computation.2.clone.1 | custom fusion | flops 1048576 | bytes 12583040 | tf_op jit(solution)/shard_map/while/body/eval_jaxpr/scatter-add | solution.py:38
  141.0 3.6 gather_fusion
  145.7 4.4 fusion.56
  150.0 6.5 %scatter_fusion = f32[16,128,256]{2,1,0:T(8,128)S(1)} fusion(f32[16,128,256]{2,1,0:T(8,128)S(1)} %get-tuple-element.232, s32[32]{0:T(128)S(1)} %get-tuple-element.213, f32[32,128,256]{2,1,0:T(8,128)} %fusion.56), kind=kCustom, calls=%fused_computation.2.clone.1 | custom fusion | flops 1048576 | bytes 12583040 | tf_op jit(solution)/shard_map/while/body/eval_jaxpr/scatter-add | solution.py:38
  157.5 3.6 gather_fusion
  162.2 4.4 fusion.56
  166.6 6.5 %scatter_fusion = f32[16,128,256]{2,1,0:T(8,128)S(1)} fusion(f32[16,128,256]{2,1,0:T(8,128)S(1)} %get-tuple-element.232, s32[32]{0:T(128)S(1)} %get-tuple-element.213, f32[32,128,256]{2,1,0:T(8,128)} %fusion.56), kind=kCustom, calls=%fused_computation.2.clone.1 | custom fusion | flops 1048576 | bytes 12583040 | tf_op jit(solution)/shard_map/while/body/eval_jaxpr/scatter-add | solution.py:38
  174.1 3.6 gather_fusion
  178.7 4.4 fusion.56
  183.1 6.5 %scatter_fusion = f32[16,128,256]{2,1,0:T(8,128)S(1)} fusion(f32[16,128,256]{2,1,0:T(8,128)S(1)} %get-tuple-element.232, s32[32]{0:T(128)S(1)} %get-tuple-element.213, f32[32,128,256]{2,1,0:T(8,128)} %fusion.56), kind=kCustom, calls=%fused_computation.2.clone.1 | custom fusion | flops 1048576 | bytes 12583040 | tf_op jit(solution)/shard_map/while/body/eval_jaxpr/scatter-add | solution.py:38
  190.6 3.6 gather_fusion
  195.3 4.4 fusion.56
  199.7 6.5 %scatter_fusion = f32[16,128,256]{2,1,0:T(8,128)S(1)} fusion(f32[16,128,256]{2,1,0:T(8,128)S(1)} %get-tuple-element.232, s32[32]{0:T(128)S(1)} %get-tuple-element.213, f32[32,128,256]{2,1,0:T(8,128)} %fusion.56), kind=kCustom, calls=%fused_computation.2.clone.1 | custom fusion | flops 1048576 | bytes 12583040 | tf_op jit(solution)/shard_map/while/body/eval_jaxpr/scatter-add | solution.py:38
  207.2 3.6 gather_fusion
  211.9 4.4 fusion.56
  216.2 6.5 %scatter_fusion = f32[16,128,256]{2,1,0:T(8,128)S(1)} fusion(f32[16,128,256]{2,1,0:T(8,128)S(1)} %get-tuple-element.232, s32[32]{0:T(128)S(1)} %get-tuple-element.213, f32[32,128,256]{2,1,0:T(8,128)} %fusion.56), kind=kCustom, calls=%fused_computation.2.clone.1 | custom fusion | flops 1048576 | bytes 12583040 | tf_op jit(solution)/shard_map/while/body/eval_jaxpr/scatter-add | solution.py:38
  223.7 3.6 gather_fusion
  228.4 4.4 fusion.56
  232.8 6.5 %scatter_fusion = f32[16,128,256]{2,1,0:T(8,128)S(1)} fusion(f32[16,128,256]{2,1,0:T(8,128)S(1)} %get-tuple-element.232, s32[32]{0:T(128)S(1)} %get-tuple-element.213, f32[32,128,256]{2,1,0:T(8,128)} %fusion.56), kind=kCustom, calls=%fused_computation.2.clone.1 | custom fusion | flops 1048576 | bytes 12583040 | tf_op jit(solution)/shard_map/while/body/eval_jaxpr/scatter-add | solution.py:38
  243.1 13.7 %all-reduce = f32[2048]{0:T(1024)S(1)} all-reduce(f32[2048]{0:T(1024)S(1)} %bitcast.96), channel_id=3, replica_groups=mesh['nodes'=16,'cols'=8] {'cols'}, use_global_device_ids=true, to_apply=%region_6.7.clone | all-reduce | flops 2048 | bytes 16384
  256.9 17.8 %reduce-scatter.3.cloned.1.call-done = f32[256,256]{1,0:T(8,128)} async-done(((f32[2048,256]{1,0:T(8,128)}), f32[256,256]{1,0:T(8,128)}) %reduce-scatter.3.cloned.1.call-update) | async-done | bytes 262160 | tf_op jit(solution)/shard_map/reduce_scatter | solution.py:50
  274.7 2.6 convert_reduce_fusion
  280.3 20.2 %all-gather.5.cloned.1.call-done = bf16[2048,256]{1,0:T(8,128)(2,1)} async-done(((bf16[256,256]{1,0:T(8,128)(2,1)}), bf16[2048,256]{1,0:T(8,128)(2,1)}) %all-gather.5.cloned.1.call-update) | async-done | bytes 1048592 | tf_op jit(solution)/shard_map/all_gather | solution.py:78
  302.9 166.3 %while.23 = (s32[]{:T(128)}, f32[32,128,256]{2,1,0:T(8,128)}, s32[11,32]{1,0:T(8,128)}, s32[11,32,16,128]{3,2,1,0:T(8,128)}, s32[11,32]{1,0:T(8,128)}, /*index=5*/bf16[16,128,256]{2,1,0:T(8,128)(2,1)S(1)}, s32[]{:T(128)}) while((s32[]{:T(128)}, f32[32,128,256]{2,1,0:T(8,128)}, s32[11,32]{1,0:T(8,128)}, s32[11,32,16,128]{3,2,1,0:T(8,128)}, ...), condition=%wide.region_9.10_spmd, body=%wide.region_7.9_spmd.sunk | while | flops 271058112 | bytes 23862236 | solution.py:88
  305.4 2.7 fusion.60
  308.1 9.9 %scatter_fusion.1 = f32[32,128,256]{2,1,0:T(8,128)} fusion(f32[32,128,256]{2,1,0:T(8,128)} %get-tuple-element.255, s32[32]{0:T(128)S(1)} %get-tuple-element.221, f32[32,128,256]{2,1,0:T(8,128)} %fusion.60), kind=kCustom, calls=%fused_computation.4.clone.1 | custom fusion | flops 1048576 | bytes 12583040 | tf_op jit(solution)/shard_map/while/body/eval_jaxpr/scatter-add | solution.py:86
  320.4 2.7 fusion.60
  323.2 9.9 %scatter_fusion.1 = f32[32,128,256]{2,1,0:T(8,128)} fusion(f32[32,128,256]{2,1,0:T(8,128)} %get-tuple-element.255, s32[32]{0:T(128)S(1)} %get-tuple-element.221, f32[32,128,256]{2,1,0:T(8,128)} %fusion.60), kind=kCustom, calls=%fused_computation.4.clone.1 | custom fusion | flops 1048576 | bytes 12583040 | tf_op jit(solution)/shard_map/while/body/eval_jaxpr/scatter-add | solution.py:86
  335.5 2.7 fusion.60
  338.3 9.9 %scatter_fusion.1 = f32[32,128,256]{2,1,0:T(8,128)} fusion(f32[32,128,256]{2,1,0:T(8,128)} %get-tuple-element.255, s32[32]{0:T(128)S(1)} %get-tuple-element.221, f32[32,128,256]{2,1,0:T(8,128)} %fusion.60), kind=kCustom, calls=%fused_computation.4.clone.1 | custom fusion | flops 1048576 | bytes 12583040 | tf_op jit(solution)/shard_map/while/body/eval_jaxpr/scatter-add | solution.py:86
  350.6 2.7 fusion.60
  353.3 9.9 %scatter_fusion.1 = f32[32,128,256]{2,1,0:T(8,128)} fusion(f32[32,128,256]{2,1,0:T(8,128)} %get-tuple-element.255, s32[32]{0:T(128)S(1)} %get-tuple-element.221, f32[32,128,256]{2,1,0:T(8,128)} %fusion.60), kind=kCustom, calls=%fused_computation.4.clone.1 | custom fusion | flops 1048576 | bytes 12583040 | tf_op jit(solution)/shard_map/while/body/eval_jaxpr/scatter-add | solution.py:86
  365.7 2.7 fusion.60
  368.4 9.9 %scatter_fusion.1 = f32[32,128,256]{2,1,0:T(8,128)} fusion(f32[32,128,256]{2,1,0:T(8,128)} %get-tuple-element.255, s32[32]{0:T(128)S(1)} %get-tuple-element.221, f32[32,128,256]{2,1,0:T(8,128)} %fusion.60), kind=kCustom, calls=%fused_computation.4.clone.1 | custom fusion | flops 1048576 | bytes 12583040 | tf_op jit(solution)/shard_map/while/body/eval_jaxpr/scatter-add | solution.py:86
  380.8 2.7 fusion.60
  383.5 10.0 %scatter_fusion.1 = f32[32,128,256]{2,1,0:T(8,128)} fusion(f32[32,128,256]{2,1,0:T(8,128)} %get-tuple-element.255, s32[32]{0:T(128)S(1)} %get-tuple-element.221, f32[32,128,256]{2,1,0:T(8,128)} %fusion.60), kind=kCustom, calls=%fused_computation.4.clone.1 | custom fusion | flops 1048576 | bytes 12583040 | tf_op jit(solution)/shard_map/while/body/eval_jaxpr/scatter-add | solution.py:86
  395.9 2.7 fusion.60
  398.7 10.2 %scatter_fusion.1 = f32[32,128,256]{2,1,0:T(8,128)} fusion(f32[32,128,256]{2,1,0:T(8,128)} %get-tuple-element.255, s32[32]{0:T(128)S(1)} %get-tuple-element.221, f32[32,128,256]{2,1,0:T(8,128)} %fusion.60), kind=kCustom, calls=%fused_computation.4.clone.1 | custom fusion | flops 1048576 | bytes 12583040 | tf_op jit(solution)/shard_map/while/body/eval_jaxpr/scatter-add | solution.py:86
  411.3 2.7 fusion.60
  414.1 9.9 %scatter_fusion.1 = f32[32,128,256]{2,1,0:T(8,128)} fusion(f32[32,128,256]{2,1,0:T(8,128)} %get-tuple-element.255, s32[32]{0:T(128)S(1)} %get-tuple-element.221, f32[32,128,256]{2,1,0:T(8,128)} %fusion.60), kind=kCustom, calls=%fused_computation.4.clone.1 | custom fusion | flops 1048576 | bytes 12583040 | tf_op jit(solution)/shard_map/while/body/eval_jaxpr/scatter-add | solution.py:86
  426.4 2.7 fusion.60
  429.1 10.0 %scatter_fusion.1 = f32[32,128,256]{2,1,0:T(8,128)} fusion(f32[32,128,256]{2,1,0:T(8,128)} %get-tuple-element.255, s32[32]{0:T(128)S(1)} %get-tuple-element.221, f32[32,128,256]{2,1,0:T(8,128)} %fusion.60), kind=kCustom, calls=%fused_computation.4.clone.1 | custom fusion | flops 1048576 | bytes 12583040 | tf_op jit(solution)/shard_map/while/body/eval_jaxpr/scatter-add | solution.py:86
  441.6 2.7 fusion.60
  444.3 9.9 %scatter_fusion.1 = f32[32,128,256]{2,1,0:T(8,128)} fusion(f32[32,128,256]{2,1,0:T(8,128)} %get-tuple-element.255, s32[32]{0:T(128)S(1)} %get-tuple-element.221, f32[32,128,256]{2,1,0:T(8,128)} %fusion.60), kind=kCustom, calls=%fused_computation.4.clone.1 | custom fusion | flops 1048576 | bytes 12583040 | tf_op jit(solution)/shard_map/while/body/eval_jaxpr/scatter-add | solution.py:86
  456.7 2.7 fusion.60
  459.4 9.8 %scatter_fusion.1 = f32[32,128,256]{2,1,0:T(8,128)} fusion(f32[32,128,256]{2,1,0:T(8,128)} %get-tuple-element.255, s32[32]{0:T(128)S(1)} %get-tuple-element.221, f32[32,128,256]{2,1,0:T(8,128)} %fusion.60), kind=kCustom, calls=%fused_computation.4.clone.1 | custom fusion | flops 1048576 | bytes 12583040 | tf_op jit(solution)/shard_map/while/body/eval_jaxpr/scatter-add | solution.py:86
  469.8 66.2 %psum.23 = f32[256]{0:T(256)} all-reduce(f32[256]{0:T(256)S(1)} %copy-done.7), channel_id=1, replica_groups=mesh['nodes'=16,'cols'=8] {'nodes','cols'}, use_global_device_ids=true, to_apply=%region_14.15 | all-reduce | flops 256 | bytes 2048 | tf_op jit(solution)/shard_map/psum | solution.py:72
  537.9 9.3 %reduce-scatter.5.cloned.1.call-done = f32[256,256]{1,0:T(8,128)} async-done(((f32[4096,256]{1,0:T(8,128)}), f32[256,256]{1,0:T(8,128)}) %reduce-scatter.5.cloned.1.call-update) | async-done | bytes 262160 | tf_op jit(solution)/shard_map/reduce_scatter | solution.py:94
  (194 shorter events, 65.4 us)
Async XLA Ops:
  7.2 267.5 %copy-start = (bf16[256,256]{1,0:T(8,128)(2,1)S(1)}, bf16[256,256]{1,0:T(8,128)(2,1)}, u32[]{:S(2)}) copy-start(bf16[256,256]{1,0:T(8,128)(2,1)} %param.17) | copy-start | bytes 393220
  7.2 50.7 %all-gather.3.cloned.1.call-start = ((), (), s32[]{:S(2)}) async-start(), calls=%async_computation.2 | async-start | bytes 2228224 | tf_op jit(solution)/shard_map/all_gather | solution.py:28
  7.9 266.8 %reduce-scatter.3.cloned.1.call-start = ((), (), s32[]{:S(2)}) async-start(), calls=%async_computation.3 | async-start | bytes 2359296 | tf_op jit(solution)/shard_map/reduce_scatter | solution.py:50
  240.2 1.4 copy-start.1
  240.2 2.0 copy-start.5
  240.2 2.0 copy-start.6
  240.3 1.4 copy-start.11
  240.3 2.6 copy-start.3
  240.3 2.6 copy-start.4
  240.3 34.4 %copy-start.9 = (bf16[256,256]{1,0:T(8,128)(2,1)S(1)}, bf16[256,256]{1,0:T(8,128)(2,1)}, u32[]{:S(2)}) copy-start(bf16[256,256]{1,0:T(8,128)(2,1)} %param.19) | copy-start | bytes 393220
  240.3 34.4 %copy-start.10 = (f32[256]{0:T(256)S(1)}, f32[256]{0:T(256)}, u32[]{:S(2)}) copy-start(f32[256]{0:T(256)} %param.18) | copy-start | bytes 3076
  241.6 58.9 %all-gather.5.cloned.1.call-start = ((), (), s32[]{:S(2)}) async-start(), calls=%async_computation.4 | async-start | bytes 1179648 | tf_op jit(solution)/shard_map/all_gather | solution.py:78
  274.7 4.5 copy-start.8
  278.2 257.9 %all-reduce.4.cloned.1.call-start = ((), (), s32[]{:S(2)}) async-start(), calls=%async_computation.6 | async-start | bytes 1048576 | tf_op jit(solution)/shard_map/psum | solution.py:72
  280.2 267.0 %reduce-scatter.5.cloned.1.call-start = ((), (), s32[]{:S(2)}) async-start(), calls=%async_computation.5 | async-start | bytes 4456448 | tf_op jit(solution)/shard_map/reduce_scatter | solution.py:94
  300.5 2.4 copy-start.2
  469.2 0.7 copy-start.7
Sparse Core Ops, SparseCore 0:
  10.2 47.7 all-gather.2
  241.7 32.9 reduce-scatter.2
  278.3 22.1 all-gather.4
  305.8 144.6 all-reduce.3
  469.3 77.8 reduce-scatter.4
where the time goes:
time: 560 us; the launch traced here: 557 us
  other arithmetic  200 us (36%)
  waiting for transfers between devices  96.4 us (17%)
  matrix products  85.6 us (15%)
  blocking collectives  80 us (14%)
  local copies, waits for them, and re-layouts  79.4 us (14%)
  between operations  14.6 us (3%)
    scatter-add x11, other arithmetic, backward_step(): return (src_grad.at[cols_blk].add(products), None)  109 us
    scatter-add x11, other arithmetic, forward_step(): summed = summed.at[rows_blk].add(products)  71.1 us
    psum x1, blocking collectives, shards(): lax.psum((self_term, neigh_term, bias_term), ('nodes', 'cols'))  66.2 us
    all_gather x1, waiting for transfers between devices, shards(): source = lax.all_gather(node_feats, 'nodes', axis=0, tiled=True)  48.4 us
    dot_general x11, matrix products, forward_step(): jnp.einsum('tba,tbf->taf', bits_blk, picked, preferred_element_type=jnp.f...  48.1 us
    gather x11, local copies, waits for them, and re-layouts, forward_step(): picked = source_blocks[cols_blk]  39.8 us
    dot_general x11, matrix products, backward_step(): jnp.einsum('tba,taf->tbf', bits_blk, picked, preferred_element_type=jnp.f...  30.1 us
    shift_right_arithmetic x66, local copies, waits for them, and re-layouts, unpack_tiles(): jnp.right_shift(packed[:, :, None, :], shifts[None, None, :, None]) & 1  23.4 us
  transfers between devices with their start and end apart: 5, of which 4 were waited for; matrix products, arithmetic and copies ran while one was open for 31% of the time, Pallas kernels for 0%

commit v1 on v0

--- a/solution.py
+++ b/solution.py
@@ -3,6 +3,7 @@
 import jax.numpy as jnp
 from jax import lax
 from jax.sharding import PartitionSpec as P
+from jax.lax import psum
 
 
 def unpack_tiles(packed):
@@ -69,8 +70,14 @@
     self_term = jnp.dot(node_feats.T, pre_grad, preferred_element_type=jnp.float32)
     neigh_term = jnp.dot(neigh_mean.T, pre_grad, preferred_element_type=jnp.float32)
     bias_term = jnp.sum(pre_grad.astype(jnp.float32), axis=0)
-    self_grad, neigh_grad, bias_grad = lax.psum(
-        (self_term, neigh_term, bias_term), ("nodes", "cols")
+
+    def run_launch(q_in, lane_axis, axis_key):
+        for dd in (lane_axis, axis_key):
+            q_in = psum(q_in, axis_name=dd)
+        return q_in
+
+    self_grad, neigh_grad, bias_grad = run_launch(
+        (self_term, neigh_term, bias_term), "cols", "nodes"
     )
     mean_grad = (
         jnp.dot(pre_grad, w_neigh.T, preferred_element_type=jnp.float32) / degree[:, None]

time: 560 us -> 624 us (1.11)
  waiting for transfers between devices: 96.4 us -> 171 us
  blocking collectives: 80 us -> 68.9 us
    psum x1 -> x2, waiting for transfers between devices: 0.01 us -> 58.7 us  [run_launch(): q_in = psum(q_in, axis_name=dd)]
    psum x1 -> x2, blocking collectives: 66.2 us -> 55.2 us  [run_launch(): q_in = psum(q_in, axis_name=dd)]
    reduce_scatter x1, waiting for transfers between devices: 9.32 us -> 20.2 us  [shards(): lax.psum_scatter(src_total, 'nodes', scatter_dimension=0, tiled=True)]
  transfers between devices with their start and end apart: 5 -> 6, of which waited for: 4 -> 5; matrix products, arithmetic and copies ran while one was open for 31% -> 28% of each run, Pallas kernels for 0% -> 0%
where the time goes in v1:
time: 624 us; the launch traced here: 621 us
  other arithmetic  200 us (32%)
  waiting for transfers between devices  171 us (27%)
  matrix products  85.6 us (14%)
  local copies, waits for them, and re-layouts  79.4 us (13%)
  blocking collectives  68.9 us (11%)
  between operations  14.9 us (2%)
    scatter-add x11, other arithmetic, backward_step(): return (src_grad.at[cols_blk].add(products), None)  109 us
    scatter-add x11, other arithmetic, forward_step(): summed = summed.at[rows_blk].add(products)  71.1 us
    psum x2, waiting for transfers between devices, run_launch(): q_in = psum(q_in, axis_name=dd)  58.7 us
    psum x2, blocking collectives, run_launch(): q_in = psum(q_in, axis_name=dd)  55.2 us
    all_gather x1, waiting for transfers between devices, shards(): source = lax.all_gather(node_feats, 'nodes', axis=0, tiled=True)  48.4 us
    dot_general x11, matrix products, forward_step(): jnp.einsum('tba,tbf->taf', bits_blk, picked, preferred_element_type=jnp.f...  48.1 us
    gather x11, local copies, waits for them, and re-layouts, forward_step(): picked = source_blocks[cols_blk]  39.8 us
    dot_general x11, matrix products, backward_step(): jnp.einsum('tba,taf->tbf', bits_blk, picked, preferred_element_type=jnp.f...  30.1 us
  transfers between devices with their start and end apart: 6, of which 5 were waited for; matrix products, arithmetic and copies ran while one was open for 28% of the time, Pallas kernels for 0%

profile of v1, /device:TPU:0, one launch (start us, length us, event | category | flops | bytes accessed | tf_op | source)
XLA Modules:
  0.0 620.7 jit_solution(4193034044587431317)
XLA Ops:
  9.5 48.4 %all-gather.3.cloned.1.call-done = bf16[4096,256]{1,0:T(8,128)(2,1)} async-done(((bf16[256,256]{1,0:T(8,128)(2,1)}), bf16[4096,256]{1,0:T(8,128)(2,1)}) %all-gather.3.cloned.1.call-update) | async-done | bytes 2097168 | tf_op jit(solution)/shard_map/all_gather | solution.py:29
  58.1 182.1 %while.22 = (s32[]{:T(128)}, f32[16,128,256]{2,1,0:T(8,128)S(1)}, f32[16,128]{1,0:T(8,128)S(1)}, s32[11,32]{1,0:T(8,128)S(1)}, s32[11,32,16,128]{3,2,1,0:T(8,128...) while((s32[]{:T(128)}, f32[16,128,256]{2,1,0:T(8,128)S(1)}, ...), condition=%wide.region_4.5_spmd, body=%wide.region_0.4_spmd.sunk | while | flops 272635072 | bytes 24165348 | solution.py:47
  58.2 3.6 gather_fusion
  62.9 4.4 fusion.56
  67.2 6.5 %scatter_fusion = f32[16,128,256]{2,1,0:T(8,128)S(1)} fusion(f32[16,128,256]{2,1,0:T(8,128)S(1)} %get-tuple-element.234, s32[32]{0:T(128)S(1)} %get-tuple-element.215, f32[32,128,256]{2,1,0:T(8,128)} %fusion.56), kind=kCustom, calls=%fused_computation.2.clone.1 | custom fusion | flops 1048576 | bytes 12583040 | tf_op jit(solution)/shard_map/while/body/eval_jaxpr/scatter-add | solution.py:39
  74.7 3.6 gather_fusion
  79.4 4.4 fusion.56
  83.8 6.5 %scatter_fusion = f32[16,128,256]{2,1,0:T(8,128)S(1)} fusion(f32[16,128,256]{2,1,0:T(8,128)S(1)} %get-tuple-element.234, s32[32]{0:T(128)S(1)} %get-tuple-element.215, f32[32,128,256]{2,1,0:T(8,128)} %fusion.56), kind=kCustom, calls=%fused_computation.2.clone.1 | custom fusion | flops 1048576 | bytes 12583040 | tf_op jit(solution)/shard_map/while/body/eval_jaxpr/scatter-add | solution.py:39
  91.3 3.6 gather_fusion
  96.0 4.4 fusion.56
  100.4 6.5 %scatter_fusion = f32[16,128,256]{2,1,0:T(8,128)S(1)} fusion(f32[16,128,256]{2,1,0:T(8,128)S(1)} %get-tuple-element.234, s32[32]{0:T(128)S(1)} %get-tuple-element.215, f32[32,128,256]{2,1,0:T(8,128)} %fusion.56), kind=kCustom, calls=%fused_computation.2.clone.1 | custom fusion | flops 1048576 | bytes 12583040 | tf_op jit(solution)/shard_map/while/body/eval_jaxpr/scatter-add | solution.py:39
  107.9 3.6 gather_fusion
  112.5 4.4 fusion.56
  116.9 6.5 %scatter_fusion = f32[16,128,256]{2,1,0:T(8,128)S(1)} fusion(f32[16,128,256]{2,1,0:T(8,128)S(1)} %get-tuple-element.234, s32[32]{0:T(128)S(1)} %get-tuple-element.215, f32[32,128,256]{2,1,0:T(8,128)} %fusion.56), kind=kCustom, calls=%fused_computation.2.clone.1 | custom fusion | flops 1048576 | bytes 12583040 | tf_op jit(solution)/shard_map/while/body/eval_jaxpr/scatter-add | solution.py:39
  124.4 3.6 gather_fusion
  129.1 4.4 fusion.56
  133.5 6.5 %scatter_fusion = f32[16,128,256]{2,1,0:T(8,128)S(1)} fusion(f32[16,128,256]{2,1,0:T(8,128)S(1)} %get-tuple-element.234, s32[32]{0:T(128)S(1)} %get-tuple-element.215, f32[32,128,256]{2,1,0:T(8,128)} %fusion.56), kind=kCustom, calls=%fused_computation.2.clone.1 | custom fusion | flops 1048576 | bytes 12583040 | tf_op jit(solution)/shard_map/while/body/eval_jaxpr/scatter-add | solution.py:39
  141.0 3.6 gather_fusion
  145.7 4.4 fusion.56
  150.0 6.5 %scatter_fusion = f32[16,128,256]{2,1,0:T(8,128)S(1)} fusion(f32[16,128,256]{2,1,0:T(8,128)S(1)} %get-tuple-element.234, s32[32]{0:T(128)S(1)} %get-tuple-element.215, f32[32,128,256]{2,1,0:T(8,128)} %fusion.56), kind=kCustom, calls=%fused_computation.2.clone.1 | custom fusion | flops 1048576 | bytes 12583040 | tf_op jit(solution)/shard_map/while/body/eval_jaxpr/scatter-add | solution.py:39
  157.5 3.6 gather_fusion
  162.2 4.4 fusion.56
  166.6 6.5 %scatter_fusion = f32[16,128,256]{2,1,0:T(8,128)S(1)} fusion(f32[16,128,256]{2,1,0:T(8,128)S(1)} %get-tuple-element.234, s32[32]{0:T(128)S(1)} %get-tuple-element.215, f32[32,128,256]{2,1,0:T(8,128)} %fusion.56), kind=kCustom, calls=%fused_computation.2.clone.1 | custom fusion | flops 1048576 | bytes 12583040 | tf_op jit(solution)/shard_map/while/body/eval_jaxpr/scatter-add | solution.py:39
  174.1 3.6 gather_fusion
  178.7 4.4 fusion.56
  183.1 6.5 %scatter_fusion = f32[16,128,256]{2,1,0:T(8,128)S(1)} fusion(f32[16,128,256]{2,1,0:T(8,128)S(1)} %get-tuple-element.234, s32[32]{0:T(128)S(1)} %get-tuple-element.215, f32[32,128,256]{2,1,0:T(8,128)} %fusion.56), kind=kCustom, calls=%fused_computation.2.clone.1 | custom fusion | flops 1048576 | bytes 12583040 | tf_op jit(solution)/shard_map/while/body/eval_jaxpr/scatter-add | solution.py:39
  190.6 3.6 gather_fusion
  195.3 4.4 fusion.56
  199.7 6.5 %scatter_fusion = f32[16,128,256]{2,1,0:T(8,128)S(1)} fusion(f32[16,128,256]{2,1,0:T(8,128)S(1)} %get-tuple-element.234, s32[32]{0:T(128)S(1)} %get-tuple-element.215, f32[32,128,256]{2,1,0:T(8,128)} %fusion.56), kind=kCustom, calls=%fused_computation.2.clone.1 | custom fusion | flops 1048576 | bytes 12583040 | tf_op jit(solution)/shard_map/while/body/eval_jaxpr/scatter-add | solution.py:39
  207.2 3.6 gather_fusion
  211.9 4.4 fusion.56
  216.2 6.5 %scatter_fusion = f32[16,128,256]{2,1,0:T(8,128)S(1)} fusion(f32[16,128,256]{2,1,0:T(8,128)S(1)} %get-tuple-element.234, s32[32]{0:T(128)S(1)} %get-tuple-element.215, f32[32,128,256]{2,1,0:T(8,128)} %fusion.56), kind=kCustom, calls=%fused_computation.2.clone.1 | custom fusion | flops 1048576 | bytes 12583040 | tf_op jit(solution)/shard_map/while/body/eval_jaxpr/scatter-add | solution.py:39
  223.7 3.6 gather_fusion
  228.4 4.4 fusion.56
  232.8 6.5 %scatter_fusion = f32[16,128,256]{2,1,0:T(8,128)S(1)} fusion(f32[16,128,256]{2,1,0:T(8,128)S(1)} %get-tuple-element.234, s32[32]{0:T(128)S(1)} %get-tuple-element.215, f32[32,128,256]{2,1,0:T(8,128)} %fusion.56), kind=kCustom, calls=%fused_computation.2.clone.1 | custom fusion | flops 1048576 | bytes 12583040 | tf_op jit(solution)/shard_map/while/body/eval_jaxpr/scatter-add | solution.py:39
  243.1 13.7 %all-reduce = f32[2048]{0:T(1024)S(1)} all-reduce(f32[2048]{0:T(1024)S(1)} %bitcast.96), channel_id=3, replica_groups=mesh['nodes'=16,'cols'=8] {'cols'}, use_global_device_ids=true, to_apply=%region_6.7.clone | all-reduce | flops 2048 | bytes 16384
  256.9 17.8 %reduce-scatter.3.cloned.1.call-done = f32[256,256]{1,0:T(8,128)} async-done(((f32[2048,256]{1,0:T(8,128)}), f32[256,256]{1,0:T(8,128)}) %reduce-scatter.3.cloned.1.call-update) | async-done | bytes 262160 | tf_op jit(solution)/shard_map/reduce_scatter | solution.py:51
  280.3 58.7 %all-reduce.8.cloned.1.call-done = (f32[256,256]{0,1:T(8,128)}, f32[256,256]{1,0:T(8,128)}) async-done(((f32[256,256]{0,1:T(8,128)}, f32[256,256]{1,0:T(8,128)}), (f32[256,256]{0,1:T(8,128)}, f32[256,256]{1,0:T(8,128)})) %all-reduce.8.cloned.1.call-update) | async-done | bytes 524304 | tf_op jit(solution)/shard_map/psum | solution.py:76
  339.0 24.8 %all-gather.5.cloned.1.call-done = bf16[2048,256]{1,0:T(8,128)(2,1)} async-done(((bf16[256,256]{1,0:T(8,128)(2,1)}), bf16[2048,256]{1,0:T(8,128)(2,1)}) %all-gather.5.cloned.1.call-update) | async-done | bytes 1048592 | tf_op jit(solution)/shard_map/all_gather | solution.py:85
  366.3 166.2 %while.23 = (s32[]{:T(128)}, f32[32,128,256]{2,1,0:T(8,128)}, s32[11,32]{1,0:T(8,128)}, s32[11,32,16,128]{3,2,1,0:T(8,128)}, s32[11,32]{1,0:T(8,128)}, /*index=5*/bf16[16,128,256]{2,1,0:T(8,128)(2,1)S(1)}, s32[]{:T(128)}) while((s32[]{:T(128)}, f32[32,128,256]{2,1,0:T(8,128)}, s32[11,32]{1,0:T(8,128)}, s32[11,32,16,128]{3,2,1,0:T(8,128)}, ...), condition=%wide.region_9.10_spmd, body=%wide.region_7.9_spmd.sunk | while | flops 271058112 | bytes 23862236 | solution.py:95
  368.8 2.7 fusion.60
  371.5 9.8 %scatter_fusion.1 = f32[32,128,256]{2,1,0:T(8,128)} fusion(f32[32,128,256]{2,1,0:T(8,128)} %get-tuple-element.257, s32[32]{0:T(128)S(1)} %get-tuple-element.223, f32[32,128,256]{2,1,0:T(8,128)} %fusion.60), kind=kCustom, calls=%fused_computation.4.clone.1 | custom fusion | flops 1048576 | bytes 12583040 | tf_op jit(solution)/shard_map/while/body/eval_jaxpr/scatter-add | solution.py:93
  383.8 2.7 fusion.60
  386.5 9.9 %scatter_fusion.1 = f32[32,128,256]{2,1,0:T(8,128)} fusion(f32[32,128,256]{2,1,0:T(8,128)} %get-tuple-element.257, s32[32]{0:T(128)S(1)} %get-tuple-element.223, f32[32,128,256]{2,1,0:T(8,128)} %fusion.60), kind=kCustom, calls=%fused_computation.4.clone.1 | custom fusion | flops 1048576 | bytes 12583040 | tf_op jit(solution)/shard_map/while/body/eval_jaxpr/scatter-add | solution.py:93
  398.9 2.7 fusion.60
  401.6 9.9 %scatter_fusion.1 = f32[32,128,256]{2,1,0:T(8,128)} fusion(f32[32,128,256]{2,1,0:T(8,128)} %get-tuple-element.257, s32[32]{0:T(128)S(1)} %get-tuple-element.223, f32[32,128,256]{2,1,0:T(8,128)} %fusion.60), kind=kCustom, calls=%fused_computation.4.clone.1 | custom fusion | flops 1048576 | bytes 12583040 | tf_op jit(solution)/shard_map/while/body/eval_jaxpr/scatter-add | solution.py:93
  416.7 9.9 %scatter_fusion.1 = f32[32,128,256]{2,1,0:T(8,128)} fusion(f32[32,128,256]{2,1,0:T(8,128)} %get-tuple-element.257, s32[32]{0:T(128)S(1)} %get-tuple-element.223, f32[32,128,256]{2,1,0:T(8,128)} %fusion.60), kind=kCustom, calls=%fused_computation.4.clone.1 | custom fusion | flops 1048576 | bytes 12583040 | tf_op jit(solution)/shard_map/while/body/eval_jaxpr/scatter-add | solution.py:93
  429.0 2.7 fusion.60
  431.8 10.0 %scatter_fusion.1 = f32[32,128,256]{2,1,0:T(8,128)} fusion(f32[32,128,256]{2,1,0:T(8,128)} %get-tuple-element.257, s32[32]{0:T(128)S(1)} %get-tuple-element.223, f32[32,128,256]{2,1,0:T(8,128)} %fusion.60), kind=kCustom, calls=%fused_computation.4.clone.1 | custom fusion | flops 1048576 | bytes 12583040 | tf_op jit(solution)/shard_map/while/body/eval_jaxpr/scatter-add | solution.py:93
  444.2 2.7 fusion.60
  446.9 10.0 %scatter_fusion.1 = f32[32,128,256]{2,1,0:T(8,128)} fusion(f32[32,128,256]{2,1,0:T(8,128)} %get-tuple-element.257, s32[32]{0:T(128)S(1)} %get-tuple-element.223, f32[32,128,256]{2,1,0:T(8,128)} %fusion.60), kind=kCustom, calls=%fused_computation.4.clone.1 | custom fusion | flops 1048576 | bytes 12583040 | tf_op jit(solution)/shard_map/while/body/eval_jaxpr/scatter-add | solution.py:93
  459.4 2.7 fusion.60
  462.1 10.1 %scatter_fusion.1 = f32[32,128,256]{2,1,0:T(8,128)} fusion(f32[32,128,256]{2,1,0:T(8,128)} %get-tuple-element.257, s32[32]{0:T(128)S(1)} %get-tuple-element.223, f32[32,128,256]{2,1,0:T(8,128)} %fusion.60), kind=kCustom, calls=%fused_computation.4.clone.1 | custom fusion | flops 1048576 | bytes 12583040 | tf_op jit(solution)/shard_map/while/body/eval_jaxpr/scatter-add | solution.py:93
  474.7 2.7 fusion.60
  477.5 9.9 %scatter_fusion.1 = f32[32,128,256]{2,1,0:T(8,128)} fusion(f32[32,128,256]{2,1,0:T(8,128)} %get-tuple-element.257, s32[32]{0:T(128)S(1)} %get-tuple-element.223, f32[32,128,256]{2,1,0:T(8,128)} %fusion.60), kind=kCustom, calls=%fused_computation.4.clone.1 | custom fusion | flops 1048576 | bytes 12583040 | tf_op jit(solution)/shard_map/while/body/eval_jaxpr/scatter-add | solution.py:93
  489.8 2.7 fusion.60
  492.5 10.0 %scatter_fusion.1 = f32[32,128,256]{2,1,0:T(8,128)} fusion(f32[32,128,256]{2,1,0:T(8,128)} %get-tuple-element.257, s32[32]{0:T(128)S(1)} %get-tuple-element.223, f32[32,128,256]{2,1,0:T(8,128)} %fusion.60), kind=kCustom, calls=%fused_computation.4.clone.1 | custom fusion | flops 1048576 | bytes 12583040 | tf_op jit(solution)/shard_map/while/body/eval_jaxpr/scatter-add | solution.py:93
  504.9 2.7 fusion.60
  507.7 9.9 %scatter_fusion.1 = f32[32,128,256]{2,1,0:T(8,128)} fusion(f32[32,128,256]{2,1,0:T(8,128)} %get-tuple-element.257, s32[32]{0:T(128)S(1)} %get-tuple-element.223, f32[32,128,256]{2,1,0:T(8,128)} %fusion.60), kind=kCustom, calls=%fused_computation.4.clone.1 | custom fusion | flops 1048576 | bytes 12583040 | tf_op jit(solution)/shard_map/while/body/eval_jaxpr/scatter-add | solution.py:93
  520.0 2.7 fusion.60
  522.7 9.8 %scatter_fusion.1 = f32[32,128,256]{2,1,0:T(8,128)} fusion(f32[32,128,256]{2,1,0:T(8,128)} %get-tuple-element.257, s32[32]{0:T(128)S(1)} %get-tuple-element.223, f32[32,128,256]{2,1,0:T(8,128)} %fusion.60), kind=kCustom, calls=%fused_computation.4.clone.1 | custom fusion | flops 1048576 | bytes 12583040 | tf_op jit(solution)/shard_map/while/body/eval_jaxpr/scatter-add | solution.py:93
  533.2 13.2 %psum.46 = f32[256]{0:T(256)S(1)} all-reduce(f32[256]{0:T(256)S(1)} %copy-done.7), channel_id=1, replica_groups=mesh['nodes'=16,'cols'=8] {'cols'}, use_global_device_ids=true, to_apply=%region_16.17 | all-reduce | flops 256 | bytes 2048 | tf_op jit(solution)/shard_map/psum | solution.py:76
  546.4 42.0 %psum.47 = f32[256]{0:T(256)} all-reduce(f32[256]{0:T(256)S(1)} %psum.46), channel_id=1, replica_groups=mesh['nodes'=16,'cols'=8] {'nodes'}, use_global_device_ids=true, to_apply=%region_17.18 | all-reduce | flops 256 | bytes 2048 | tf_op jit(solution)/shard_map/psum | solution.py:76
  590.2 20.2 %reduce-scatter.5.cloned.1.call-done = f32[256,256]{1,0:T(8,128)} async-done(((f32[4096,256]{1,0:T(8,128)}), f32[256,256]{1,0:T(8,128)}) %reduce-scatter.5.cloned.1.call-update) | async-done | bytes 262160 | tf_op jit(solution)/shard_map/reduce_scatter | solution.py:101
  (198 shorter events, 70.7 us)
Async XLA Ops:
  7.2 267.5 %copy-start = (bf16[256,256]{1,0:T(8,128)(2,1)S(1)}, bf16[256,256]{1,0:T(8,128)(2,1)}, u32[]{:S(2)}) copy-start(bf16[256,256]{1,0:T(8,128)(2,1)} %param.17) | copy-start | bytes 393220
  7.2 50.7 %all-gather.3.cloned.1.call-start = ((), (), s32[]{:S(2)}) async-start(), calls=%async_computation.2 | async-start | bytes 2228224 | tf_op jit(solution)/shard_map/all_gather | solution.py:29
  7.9 266.8 %reduce-scatter.3.cloned.1.call-start = ((), (), s32[]{:S(2)}) async-start(), calls=%async_computation.3 | async-start | bytes 2359296 | tf_op jit(solution)/shard_map/reduce_scatter | solution.py:51
  240.2 1.4 copy-start.1
  240.2 2.0 copy-start.5
  240.2 2.0 copy-start.6
  240.3 1.4 copy-start.11
  240.3 2.6 copy-start.3
  240.3 2.6 copy-start.4
  240.3 34.4 %copy-start.9 = (bf16[256,256]{1,0:T(8,128)(2,1)S(1)}, bf16[256,256]{1,0:T(8,128)(2,1)}, u32[]{:S(2)}) copy-start(bf16[256,256]{1,0:T(8,128)(2,1)} %param.19) | copy-start | bytes 393220
  240.3 34.4 %copy-start.10 = (f32[256]{0:T(256)S(1)}, f32[256]{0:T(256)}, u32[]{:S(2)}) copy-start(f32[256]{0:T(256)} %param.18) | copy-start | bytes 3076
  241.6 97.4 %all-reduce.8.cloned.1.call-start = ((), (), s32[]{:S(2)}) async-start(), calls=%async_computation.7 | async-start | bytes 1048576 | tf_op jit(solution)/shard_map/psum | solution.py:76
  274.7 3.5 copy-start.8
  279.3 84.6 %all-gather.5.cloned.1.call-start = ((), (), s32[]{:S(2)}) async-start(), calls=%async_computation.4 | async-start | bytes 1179648 | tf_op jit(solution)/shard_map/all_gather | solution.py:85
  280.2 308.2 %all-reduce.6.cloned.1.call-start = ((), (), s32[]{:S(2)}) async-start(), calls=%async_computation.6 | async-start | bytes 1048576 | tf_op jit(solution)/shard_map/psum | solution.py:76
  339.0 271.3 %reduce-scatter.5.cloned.1.call-start = ((), (), s32[]{:S(2)}) async-start(), calls=%async_computation.5 | async-start | bytes 4456448 | tf_op jit(solution)/shard_map/reduce_scatter | solution.py:101
  363.9 2.4 copy-start.2
  532.5 0.7 copy-start.7
Sparse Core Ops, SparseCore 0:
  10.2 47.7 all-gather.2
  241.7 32.9 reduce-scatter.2
  279.4 59.5 all-reduce.7
  341.2 22.5 all-gather.4
  367.4 85.2 all-reduce.5
  532.7 77.6 reduce-scatter.4
